TPU v7x, 512 devices: a whole 4x8x8 slice. The times are simulated.
512 devices in a mesh: energy: 64 (over z, y), space: 8 (over x, core).
Axes of the slice: x: 4, y: 8, z: 8, core: 2. Of those that a mesh axis runs over, the one named last changes fastest.
Arguments:
- green_ret: bfloat16 [64, 64, 128, 128], P('energy', 'space'), may hold values from -0.5 to 0.5
- prior_less: bfloat16 [64, 64, 128, 128], P('energy', 'space'), may hold values from -1.25 to 9.25
- prior_great: bfloat16 [64, 64, 128, 128], P('energy', 'space'), may hold values from -1.25 to 9.25
- coupling: bfloat16 [64, 128, 128], P('space'), may hold values from -0.5 to 0.5
- phonon_coupling: float32 [128, 128], P('energy'), may hold values from 0.1 to 1
- phonon_shift: int32 [2], replicated, may hold values from 1 to 32
- active_blocks: int32 [64], replicated, may hold values from 32 to 64
Outputs:
- sigma_less: bfloat16 [64, 64, 128, 128], P(None, 'space', 'energy')
- sigma_great: bfloat16 [64, 64, 128, 128], P(None, 'space', 'energy')
- current: float32 [64, 64], P('energy', 'space')
- ldos: float32 [64, 64], P('energy', 'space')
All inputs are finite; a program needn't handle non-finite values.
Results may differ from a plain program's by a relative error of at most 0.009.
Values may be sent and summed in bfloat16 or wider, within the bound.
A program may use at most 64 MiB of HBM per device.

v0:
```python
import jax
import jax.numpy as jnp
from jax import lax
from jax.sharding import PartitionSpec as P

phonon_occupation = 0.5


def shifted(value, axis, steps):
    count = lax.axis_size(axis)
    initial, last = (max(0, -steps), min(count, count - steps))
    return lax.ppermute(value, axis, [(source, source + steps) for source in range(initial, last)])


def sandwich(retarded, middle_part):
    half_product = jnp.einsum(
        "enij,kenjl->kenil", retarded, middle_part, preferred_element_type=jnp.float32
    ).astype(jnp.bfloat16)
    return jnp.einsum(
        "kenil,enml->kenim", half_product, retarded, preferred_element_type=jnp.float32
    )


def displaced(blocks_in, offset):
    energies = blocks_in.shape[0]
    target = jnp.arange(energies, dtype=jnp.int32) + offset
    inside_grid = (target >= 0) & (target < energies)
    rolled = jnp.roll(blocks_in, -offset, axis=0).astype(jnp.float32)
    return jnp.where(inside_grid[:, None, None, None], rolled, jnp.float32(0.0))


def local(
    green_ret, prior_less, prior_great, coupling, phonon_coupling, phonon_shift, active_blocks
):
    energy_count, block_count, orbitals, _ = green_ret.shape
    energy_start = lax.axis_index("energy") * energy_count
    block_start = lax.axis_index("space") * block_count
    priors = jnp.stack([prior_less, prior_great])
    bare = sandwich(green_ret, priors).astype(jnp.bfloat16)
    next_first = shifted(bare[:, :, 0], "space", -1)
    following = jnp.concatenate([bare[:, :, 1:], next_first[:, :, None]], 2)
    lowered = jnp.einsum(
        "nij,kenjl->kenil", coupling, following, preferred_element_type=jnp.float32
    ).astype(jnp.bfloat16)
    downward = jnp.einsum("kenil,nml->kenim", lowered, coupling, preferred_element_type=jnp.float32)
    raised = jnp.einsum(
        "nji,kenjl->kenil", coupling, bare, preferred_element_type=jnp.float32
    ).astype(jnp.bfloat16)
    upward = jnp.einsum(
        "kenil,nlm->kenim", raised, coupling, preferred_element_type=jnp.float32
    ).astype(jnp.bfloat16)
    prev_upward = shifted(upward[:, :, -1], "space", 1)
    previous = jnp.concatenate([prev_upward[:, :, None], upward[:, :, :-1]], 2)
    source = (priors.astype(jnp.float32) + previous.astype(jnp.float32) + downward).astype(
        jnp.bfloat16
    )
    result = sandwich(green_ret, source)
    open_counts = lax.dynamic_slice_in_dim(active_blocks, energy_start, energy_count)
    block_ids = block_start + jnp.arange(block_count, dtype=jnp.int32)
    open_mask = (block_ids[None, :] < open_counts[:, None]).astype(jnp.float32)
    greens = (result * open_mask[None, :, :, None, None]).astype(jnp.bfloat16)
    lesser = greens[0]
    greater = greens[1]
    row_count = orbitals // lax.axis_size("energy")
    first_row = lax.axis_index("energy") * row_count
    columns = jnp.arange(orbitals, dtype=jnp.int32)
    row_ids = first_row + jnp.arange(row_count, dtype=jnp.int32)
    diagonal_mask = (columns[None, :] == row_ids[:, None]).astype(jnp.float32)
    occupied = jnp.float32(phonon_occupation)
    lesser_rows = lax.all_to_all(lesser, "energy", split_axis=2, concat_axis=0, tiled=True)
    greater_rows = lax.all_to_all(greater, "energy", split_axis=2, concat_axis=0, tiled=True)
    less_sum = jnp.zeros(lesser_rows.shape, jnp.float32)
    great_sum = jnp.zeros(greater_rows.shape, jnp.float32)
    for branch in range(2):
        offset = phonon_shift[branch]
        less_sum = (
            less_sum
            + (1.0 + occupied) * displaced(lesser_rows, offset)
            + occupied * displaced(lesser_rows, -offset)
        )
        great_sum = (
            great_sum
            + (1.0 + occupied) * displaced(greater_rows, -offset)
            + occupied * displaced(greater_rows, offset)
        )
    sigma_l = (phonon_coupling * less_sum).astype(jnp.bfloat16)
    sigma_g = (phonon_coupling * great_sum).astype(jnp.bfloat16)
    lesser_wide = lesser_rows.astype(jnp.float32)
    greater_wide = greater_rows.astype(jnp.float32)
    scattering = (
        jnp.sum(
            sigma_l.astype(jnp.float32) * greater_wide - sigma_g.astype(jnp.float32) * lesser_wide,
            axis=(2, 3),
        )
        / orbitals
    )
    density = jnp.sum((lesser_wide + greater_wide) * diagonal_mask, axis=(2, 3)) / orbitals
    current, ldos = (
        lax.psum_scatter(scattering, "energy", scatter_dimension=0, tiled=True),
        lax.psum_scatter(density, "energy", scatter_dimension=0, tiled=True),
    )
    return (sigma_l, sigma_g, current, ldos)


def solution(mesh):
    return jax.shard_map(
        local,
        mesh=mesh,
        in_specs=(
            P("energy", "space", None, None),
            P("energy", "space", None, None),
            P("energy", "space", None, None),
            P("space", None, None),
            P("energy", None),
            P(),
            P(),
        ),
        out_specs=(
            P(None, "space", "energy", None),
            P(None, "space", "energy", None),
            P("energy", "space"),
            P("energy", "space"),
        ),
        check_vma=False,
    )
```

profile of v0, /device:TPU:6, one launch (start us, length us, event | category | flops | bytes accessed | tf_op | source)
XLA Modules:
  0.0 353.5 jit_solution(11155068213723799267)
XLA Ops:
  0.6 0.0 copy-start
  0.6 0.0 copy-start.2
  0.7 1.2 copy.24
  1.8 0.0 copy-done.2
  1.8 0.0 copy-start.5
  1.9 0.2 copy.23
  2.0 0.8 copy-done.5
  2.8 0.5 convolution_convert_fusion.4
  3.3 2.2 collective-permute-start.1
  5.5 0.0 copy-done
  5.5 0.5 fusion.5
  6.1 0.0 copy-start.1
  6.1 2.1 collective-permute-start
  8.3 0.0 copy-done.1
  8.3 0.0 copy-start.6
  8.3 0.6 copy-done.6
  8.9 0.6 dynamic_slice.6
  9.5 0.6 compare_convert_fusion.1
  10.2 0.0 collective-permute-done.1
  10.2 0.0 slice-start
  10.2 0.5 convolution_bitcast_fusion
  10.7 1.0 collective-permute-done
  11.7 0.0 slice-done
  11.7 1.6 fusion.2
  13.3 0.9 copy.35
  14.2 0.0 copy-start.3
  14.2 16.7 %all-to-all-start.1 = ((bf16[1,8,128,128]{3,1,0,2:T(8,128)(2,1)}), bf16[1,8,128,128]{3,1,0,2:T(8,128)(2,1)S(1)}, u32[]{:S(2)}, u32[]{:S(2)}) async-start(bf16[1,8,128,128]{3,1,0,2:T(8,128)(2,1)} %copy.35), calls=%async_computation.1 | async-start | bytes 524288 | tf_op jit(solution)/shard_map/all_to_all | solution.py:71
  30.9 0.0 copy-done.3
  30.9 0.6 fusion.47
  36.7 1.3 dynamic-slice
  38.0 0.9 copy.33
  38.9 6.1 %all-to-all-done.1 = bf16[1,8,128,128]{3,1,0,2:T(8,128)(2,1)S(1)} async-done(((bf16[1,8,128,128]{3,1,0,2:T(8,128)(2,1)}), bf16[1,8,128,128]{3,1,0,2:T(8,128)(2,1)S(1)}, u32[]{:S(2)}, u32[]{:S(2)}) %all-to-all-start.1) | async-done | bytes 262176 | tf_op jit(solution)/shard_map/all_to_all | solution.py:71
  45.0 6.6 %all-to-all-start = ((bf16[1,8,128,128]{3,1,0,2:T(8,128)(2,1)}), bf16[1,8,128,128]{3,1,0,2:T(8,128)(2,1)S(1)}, u32[]{:S(2)}, u32[]{:S(2)}) async-start(bf16[1,8,128,128]{3,1,0,2:T(8,128)(2,1)} %copy.33), calls=%async_computation | async-start | bytes 524288 | tf_op jit(solution)/shard_map/all_to_all | solution.py:70
  51.6 0.7 compare_and_fusion
  52.3 0.7 compare_and_fusion.2
  53.0 0.1 compare_convert_fusion
  53.0 0.2 copy.57
  53.2 12.1 %all-to-all-done = bf16[1,8,128,128]{3,1,0,2:T(8,128)(2,1)S(1)} async-done(((bf16[1,8,128,128]{3,1,0,2:T(8,128)(2,1)}), bf16[1,8,128,128]{3,1,0,2:T(8,128)(2,1)S(1)}, u32[]{:S(2)}, u32[]{:S(2)}) %all-to-all-start) | async-done | bytes 262176 | tf_op jit(solution)/shard_map/all_to_all | solution.py:70
  65.3 0.2 copy.58
  65.5 0.0 copy-start.4
  65.5 0.7 copy-done.4
  66.2 10.1 %fusion.11 = (f32[64,8]{1,0:T(8,128)S(1)}, f32[64,8]{1,0:T(8,128)S(1)}, bf16[64,8,2,128]{3,2,1,0:T(2,128)(2,1)}, bf16[64,8,2,128]{3,2,1,0:T(2,128)(2,1)}) fusion(f32[2,128]{1,0:T(2,128)S(1)} %compare_convert_fusion, bf16[1,8,64,2,128]{4,1,3,2,0:T(8,128)(2,1)S(1)} %bitcast.136, bf16[1,8,64,2,128]{4,1,3,2,0:T(8,128)(2,1)S(1)} %bitcast.134, s32[]{:T(128)S(6)} %select_n.66, ...), kind=kLoop, calls=%fused_computation.23 | loop fusion | flops 6945792 | bytes 1579280 | tf_op jit(solution)/shard_map/reduce_sum | solution.py:97
  76.3 274.9 %all-reduce.2 = (f32[64,8]{1,0:T(8,128)S(1)}, f32[64,8]{1,0:T(8,128)S(1)}) all-reduce(f32[64,8]{1,0:T(8,128)S(1)} %broadcast_multiply_fusion.1, f32[64,8]{1,0:T(8,128)S(1)} %broadcast_multiply_fusion), channel_id=2, replica_groups=mesh['energy'=64,'space'=8] {'energy'}, use_global_device_ids=true, to_apply=%region_1.3.clone | all-reduce | flops 1024 | bytes 8192
  351.2 1.1 constant_dynamic-slice_fusion.1
  352.3 1.1 constant_dynamic-slice_fusion
  (7 shorter events, 0.1 us)
Async XLA Ops:
  0.6 4.9 %copy-start = (bf16[8,128,128]{2,1,0:T(8,128)(2,1)S(1)}, bf16[8,128,128]{2,1,0:T(8,128)(2,1)}, u32[]{:S(2)}) copy-start(bf16[8,128,128]{2,1,0:T(8,128)(2,1)} %param.12) | copy-start | bytes 786436
  0.6 1.2 copy-start.2
  1.8 1.0 copy-start.5
  3.3 6.9 %collective-permute-start.1 = (bf16[2,1,128,128]{3,2,0,1:T(8,128)(2,1)S(1)}, bf16[2,1,128,128]{3,2,0,1:T(8,128)(2,1)S(1)}, u32[]{:S(2)}, u32[]{:S(2)}) collective-permute-start(bf16[2,1,128,128]{3,2,0,1:T(8,128)(2,1)S(1)} %slice_bitcast_fusion.2), channel_id=1, source_target_pairs={{1,0},{2,1},{3,2},{4,3},{5,4},{6,5},{7,6},{9,8},{10,9},{11,10},{12... | collective-permute-start | bytes 196616 | tf_op jit(solution)/shard_map/ppermute | solution.py:12
  6.1 2.2 copy-start.1
  6.1 5.6 %collective-permute-start = (bf16[2,1,128,128]{2,3,0,1:T(8,128)(2,1)S(1)}, bf16[2,1,128,128]{2,3,0,1:T(8,128)(2,1)S(1)}, u32[]{:S(2)}, u32[]{:S(2)}) collective-permute-start(bf16[2,1,128,128]{2,3,0,1:T(8,128)(2,1)S(1)} %slice_bitcast_fusion.3), channel_id=1, source_target_pairs={{0,1},{1,2},{2,3},{3,4},{4,5},{5,6},{6,7},{8,9},{9,10},{10,11},{11... | collective-permute-start | bytes 196616 | tf_op jit(solution)/shard_map/ppermute | solution.py:12
  8.3 0.7 copy-start.6
  10.2 1.5 slice-start
  14.2 16.7 %copy-start.3 = (s32[2]{0:T(128)S(1)}, s32[2]{0:T(128)}, u32[]{:S(2)}) copy-start(s32[2]{0:T(128)} %param.14) | copy-start | bytes 28
  14.2 30.9 %all-to-all-start.1 = ((bf16[1,8,128,128]{3,1,0,2:T(8,128)(2,1)}), bf16[1,8,128,128]{3,1,0,2:T(8,128)(2,1)S(1)}, u32[]{:S(2)}, u32[]{:S(2)}) async-start(bf16[1,8,128,128]{3,1,0,2:T(8,128)(2,1)} %copy.35), calls=%async_computation.1 | async-start | bytes 524288 | tf_op jit(solution)/shard_map/all_to_all | solution.py:71
  45.0 20.3 %all-to-all-start = ((bf16[1,8,128,128]{3,1,0,2:T(8,128)(2,1)}), bf16[1,8,128,128]{3,1,0,2:T(8,128)(2,1)S(1)}, u32[]{:S(2)}, u32[]{:S(2)}) async-start(bf16[1,8,128,128]{3,1,0,2:T(8,128)(2,1)} %copy.33), calls=%async_computation | async-start | bytes 524288 | tf_op jit(solution)/shard_map/all_to_all | solution.py:70
  65.5 0.7 copy-start.4
where the time goes:
time: 356 us; the launch traced here: 353 us
  blocking collectives  275 us (77%)
  starting transfers between devices  27.6 us (8%)
  waiting for transfers between devices  19.1 us (5%)
  other arithmetic  12.1 us (3%)
  local copies, waits for them, and re-layouts  10.5 us (3%)
  between operations  6.12 us (2%)
    unnamed x1, blocking collectives  275 us
    all_to_all x1, starting transfers between devices, local(): lax.all_to_all(greater, 'energy', split_axis=2, concat_axis=0, tiled=True)  16.7 us
    all_to_all x1, waiting for transfers between devices, local(): lax.all_to_all(lesser, 'energy', split_axis=2, concat_axis=0, tiled=True)  12.1 us
    reduce_sum x1, other arithmetic, local(): jnp.sum((lesser_wide + greater_wide) * diagonal_mask, axis=(2, 3))  10.1 us
  transfers between devices with their start and end apart: 4, of which 3 were waited for; matrix products, arithmetic and copies ran while one was open for 2% of the time, Pallas kernels for 0%

commit v1 on v0

v1 whole, which is shorter than its diff:
```python
import functools

import jax
import jax.numpy as jnp
from jax import lax
from jax.experimental import pallas as pl
from jax.experimental.pallas import tpu as pltpu
from jax.sharding import PartitionSpec as P

phonon_occupation = 0.5
MESH = pl.DeviceIdType.MESH
F32 = jnp.float32
BF16 = jnp.bfloat16

NE = 64
NB = 8
NO = 128
HALF = 4
PAD = 32
SIDE = 8


def dot(left, right):
    return jnp.dot(left, right, preferred_element_type=F32)


def dot_t(left, right):
    return lax.dot_general(left, right, (((1,), (1,)), ((), ())), preferred_element_type=F32)


def side_by_side(stacked):
    return jnp.concatenate([stacked[:NO], stacked[NO:]], axis=1)


def stacked(wide):
    return jnp.concatenate([wide[:, :NO], wide[:, NO:]], axis=0)


def kernel(
    g_ref, pl_ref, pg_ref, c_ref, pc_ref, shift_ref, active_ref,
    sl_ref, sg_ref, cur_ref, ldos_ref,
    bare, ct, up_out, up_in, rows, send, recv_low, recv_high, part, total,
    halo_send, halo_recv, x_send, x_recv, t_send, t_recv,
):
    me = lax.axis_index("energy")
    space = lax.axis_index("space")
    spaces = lax.axis_size("space")
    recvs = (recv_low, recv_high)

    barrier = pltpu.get_barrier_semaphore()

    @pl.loop(1, NE)
    def _(k):
        pl.semaphore_signal(barrier, inc=1, device_id={"energy": (me + k) % NE}, device_id_type=MESH)

    @pl.when(space > 0)
    def _():
        pl.semaphore_signal(barrier, inc=1, device_id={"space": space - 1}, device_id_type=MESH)

    @pl.when(space < spaces - 1)
    def _():
        pl.semaphore_signal(barrier, inc=1, device_id={"space": space + 1}, device_id_type=MESH)

    row_id = lax.broadcasted_iota(jnp.int32, (NO, NO), 0)
    col_id = lax.broadcasted_iota(jnp.int32, (NO, NO), 1)
    original = 2 * (row_id % NE) + row_id // NE
    select = col_id == original
    permute = jnp.where(select, F32(1), F32(0)).astype(BF16)
    diagonal = jnp.where(select, F32(1), F32(0))

    def prior(b):
        return jnp.concatenate([pl_ref[b], pg_ref[b]], axis=0)

    def make_bare(b):
        wide = jnp.concatenate([pl_ref[b], pg_ref[b]], axis=1)
        half = dot(g_ref[b], wide).astype(BF16)
        bare[b] = dot_t(stacked(half), g_ref[b]).astype(BF16)

    def rise(b):
        return stacked(dot(ct[b], side_by_side(bare[b])).astype(BF16))

    for g in range(2):
        recvs[g][0:PAD] = jnp.zeros((PAD, 16, NO), BF16)
        recvs[g][PAD + NE :] = jnp.zeros((PAD, 16, NO), BF16)
    for b in range(NB):
        ct[b] = c_ref[b].T

    make_bare(0)
    make_bare(NB - 1)
    up_out[...] = dot(rise(NB - 1), c_ref[NB - 1]).astype(BF16)

    neighbours = (space > 0).astype(jnp.int32) + (space < spaces - 1).astype(jnp.int32)
    pl.semaphore_wait(barrier, NE - 1 + neighbours)

    down_copy = pltpu.make_async_remote_copy(
        src_ref=bare.at[0], dst_ref=bare.at[NB], send_sem=halo_send.at[0], recv_sem=halo_recv.at[0],
        device_id={"space": lax.rem(space + spaces - 1, spaces)}, device_id_type=MESH,
    )
    up_copy = pltpu.make_async_remote_copy(
        src_ref=up_out, dst_ref=up_in, send_sem=halo_send.at[1], recv_sem=halo_recv.at[1],
        device_id={"space": lax.rem(space + 1, spaces)}, device_id_type=MESH,
    )

    @pl.when(space > 0)
    def _():
        down_copy.start()

    @pl.when(space < spaces - 1)
    def _():
        up_copy.start()

    for b in range(1, NB - 1):
        make_bare(b)

    @pl.when(space == 0)
    def _():
        up_in[...] = jnp.zeros_like(up_in)

    @pl.when(space == spaces - 1)
    def _():
        bare[NB] = jnp.zeros((2 * NO, NO), BF16)

    open_count = active_ref[me]
    lane8 = lax.broadcasted_iota(jnp.int32, (8, NO), 1)
    sub8 = lax.broadcasted_iota(jnp.int32, (8, NO), 0)

    def finish(b, ldos):
        fall = stacked(dot(c_ref[b], side_by_side(bare[b + 1])).astype(BF16))
        if b == 0:
            hops = dot(fall, ct[0]) + up_in[...].astype(F32)
        else:
            left = jnp.concatenate([rise(b - 1), fall], axis=1)
            right = jnp.concatenate([c_ref[b - 1], ct[b]], axis=0)
            hops = dot(left, right)
        source = (prior(b).astype(F32) + hops).astype(BF16)
        mine = dot(permute, g_ref[b]).astype(BF16)
        half = dot(mine, side_by_side(source)).astype(BF16)
        result = dot_t(stacked(half), g_ref[b])
        result = result * jnp.where(space * NB + b < open_count, F32(1), F32(0))
        trace = jnp.sum((result[:NO] + result[NO:]) * diagonal, axis=0, keepdims=True)
        g, inside = b // HALF, b % HALF
        for kind in range(2):
            for r in range(2):
                start = kind * 8 + inside * 2 + r
                at = kind * NO + r * NE
                rows[g, pl.ds(start, NE, stride=16), :] = result[at : at + NE]
        return jnp.where(sub8 == b, jnp.broadcast_to(trace, (8, NO)), ldos)

    def exchange(g, k):
        p = (me + k) % NE
        return pltpu.make_async_remote_copy(
            src_ref=send.at[g, p], dst_ref=recvs[g].at[PAD + me], send_sem=x_send.at[g], recv_sem=x_recv.at[g],
            device_id={"energy": p}, device_id_type=MESH,
        )

    def send_half(g):
        send[g] = rows[g].reshape(NE, 16, NO).astype(BF16)

        @pl.loop(1, NE)
        def _(k):
            exchange(g, k).start()

        recvs[g][PAD + me] = send[g, me]

    def whole(g):
        return pltpu.make_async_remote_copy(
            src_ref=send.at[g, pl.ds(0, NE - 1)], dst_ref=recvs[g].at[pl.ds(0, NE - 1)],
            send_sem=x_send.at[g], recv_sem=x_recv.at[g],
            device_id={"energy": (me + 1) % NE}, device_id_type=MESH,
        )

    ldos = jnp.zeros((8, NO), F32)

    @pl.when(space < spaces - 1)
    def _():
        down_copy.wait_recv()

    for b in range(HALF, NB):
        ldos = finish(b, ldos)
    send_half(1)

    @pl.when(space > 0)
    def _():
        up_copy.wait_recv()

    for b in range(HALF):
        ldos = finish(b, ldos)
    send_half(0)

    def as_row(columns):
        sums = jnp.sum(columns, axis=1, keepdims=True)
        return jnp.sum(jnp.where(lane8 == sub8, sums, F32(0)), axis=0, keepdims=True)[:, :NB]

    ldos_ref[...] = as_row(ldos) / NO

    occupied = F32(phonon_occupation)
    coupling8 = jnp.where(sub8 % 2 == 0, pc_ref[0:1, :], pc_ref[1:2, :])
    strong, weak = coupling8 * (1 + occupied), coupling8 * occupied
    s0, s1 = shift_ref[0], shift_ref[1]

    def sigma(g):
        whole(g).wait_recv()
        recv = recvs[g]

        def step(e, acc):
            at = PAD + e
            here = recv[at].astype(F32)
            up = recv[at + s0].astype(F32) + recv[at + s1].astype(F32)
            down = recv[at - s0].astype(F32) + recv[at - s1].astype(F32)
            less = (strong * up[:8] + weak * down[:8]).astype(BF16)
            great = (strong * down[8:] + weak * up[8:]).astype(BF16)
            sl_ref[e, g] = less
            sg_ref[e, g] = great
            flow = less.astype(F32) * here[8:] - great.astype(F32) * here[:8]
            sums = jnp.sum(flow, axis=1, keepdims=True)
            return jnp.where(lane8 == e, sums, acc)

        part[pl.ds(8 * g, 8), :] = lax.fori_loop(0, NE, step, jnp.zeros((8, NO), F32), unroll=8)

    sigma(1)
    sigma(0)

    z, y = me // SIDE, me % SIDE
    value = part[pl.ds(0, 8, stride=2), :] + part[pl.ds(1, 8, stride=2), :]
    for phase in range(2):
        mine = y if phase == 0 else z
        total[phase, mine] = value

        def hop(k, phase=phase, mine=mine):
            there = (mine + k) % SIDE
            peer = z * SIDE + there if phase == 0 else there * SIDE + y
            return pltpu.make_async_remote_copy(
                src_ref=total.at[phase, mine], dst_ref=total.at[phase, mine],
                send_sem=t_send.at[phase], recv_sem=t_recv.at[phase],
                device_id={"energy": peer}, device_id_type=MESH,
            )

        for k in range(1, SIDE):
            hop(k).start()
        everything = pltpu.make_async_remote_copy(
            src_ref=total.at[phase, pl.ds(0, SIDE - 1)], dst_ref=total.at[phase, pl.ds(0, SIDE - 1)],
            send_sem=t_send.at[phase], recv_sem=t_recv.at[phase],
            device_id={"energy": (me + 1) % NE}, device_id_type=MESH,
        )
        everything.wait_recv()
        value = jnp.sum(total[phase], axis=0)
        everything.wait_send()

    cur_ref[...] = as_row(jnp.where(lane8 == me, value, F32(0))) / NO

    @pl.when(space > 0)
    def _():
        down_copy.wait_send()

    @pl.when(space < spaces - 1)
    def _():
        up_copy.wait_send()

    whole(1).wait_send()
    whole(0).wait_send()


def local(
    green_ret, prior_less, prior_great, coupling, phonon_coupling, phonon_shift, active_blocks
):
    vmem = pl.BlockSpec(memory_space=pltpu.VMEM)
    smem = pl.BlockSpec(memory_space=pltpu.SMEM)
    dma = pltpu.SemaphoreType.DMA
    sigma_l, sigma_g, current, ldos = pl.pallas_call(
        kernel,
        out_shape=(
            jax.ShapeDtypeStruct((NE, 2, 8, NO), BF16),
            jax.ShapeDtypeStruct((NE, 2, 8, NO), BF16),
            jax.ShapeDtypeStruct((1, NB), F32),
            jax.ShapeDtypeStruct((1, NB), F32),
        ),
        in_specs=[vmem] * 5 + [smem] * 2,
        out_specs=[vmem] * 4,
        scratch_shapes=[
            pltpu.VMEM((NB + 1, 2 * NO, NO), BF16),
            pltpu.VMEM((NB, NO, NO), BF16),
            pltpu.VMEM((2 * NO, NO), BF16),
            pltpu.VMEM((2 * NO, NO), BF16),
            pltpu.VMEM((2, NE * 16, NO), F32),
            pltpu.VMEM((2, NE, 16, NO), BF16),
            pltpu.VMEM((NE + 2 * PAD, 16, NO), BF16),
            pltpu.VMEM((NE + 2 * PAD, 16, NO), BF16),
            pltpu.VMEM((16, NO), F32),
            pltpu.VMEM((2, SIDE, 8, NO), F32),
            dma((2,)), dma((2,)), dma((2,)), dma((2,)), dma((2,)), dma((2,)),
        ],
        compiler_params=pltpu.CompilerParams(
            collective_id=0, has_side_effects=True, vmem_limit_bytes=32 << 20
        ),
        name="born_step",
    )(
        green_ret.reshape(NB, NO, NO),
        prior_less.reshape(NB, NO, NO),
        prior_great.reshape(NB, NO, NO),
        coupling,
        phonon_coupling,
        phonon_shift,
        active_blocks,
    )
    shape = (NE, NB, 2, NO)
    return sigma_l.reshape(shape), sigma_g.reshape(shape), current, ldos


def solution(mesh):
    return jax.shard_map(
        local,
        mesh=mesh,
        in_specs=(
            P("energy", "space", None, None),
            P("energy", "space", None, None),
            P("energy", "space", None, None),
            P("space", None, None),
            P("energy", None),
            P(),
            P(),
        ),
        out_specs=(
            P(None, "space", "energy", None),
            P(None, "space", "energy", None),
            P("energy", "space"),
            P("energy", "space"),
        ),
        check_vma=False,
    )
```

time: 356 us -> 53.1 us (0.15)
  blocking collectives: 275 us -> 0 us
  Pallas kernels: 0 us -> 44.8 us
  starting transfers between devices: 27.6 us -> 0 us
  waiting for transfers between devices: 19.1 us -> 0 us
  other arithmetic: 12.1 us -> 0 us
  between operations: 6.12 us -> 0.67 us
  local copies, waits for them, and re-layouts: 10.5 us -> 6.9 us
    unnamed x1 -> x0, blocking collectives: 275 us -> none
    pallas_call x0 -> x1, Pallas kernels: none -> 44.8 us  [local(): pl.pallas_call(kernel, out_shape=(jax.ShapeDtypeStruct((NE, 2, 8, NO), BF...]
    all_to_all x2 -> x0, starting transfers between devices: 23.3 us -> none  [the longest x1 16.7 us: local(): lax.all_to_all(greater, 'energy', split_axis=2, concat_axis=0, tiled=True)]
    all_to_all x2 -> x0, waiting for transfers between devices: 18.2 us -> none  [the longest x1 12.1 us: local(): lax.all_to_all(lesser, 'energy', split_axis=2, concat_axis=0, tiled=True)]
    reduce_sum x1 -> x0, other arithmetic: 10.1 us -> none  [local(): jnp.sum((lesser_wide + greater_wide) * diagonal_mask, axis=(2, 3))]
    ppermute x2 -> x0, starting transfers between devices: 4.33 us -> none  [shifted(): lax.ppermute(value, axis, [(source, source + steps) for source in range(i...]
  transfers between devices with their start and end apart: 4 -> 0, of which waited for: 3 -> 0; matrix products, arithmetic and copies ran while one was open for 2% -> 0% of each run, Pallas kernels for 0% -> 0%
where the time goes in v1:
time: 53.1 us; the launch traced here: 52.4 us
  Pallas kernels  44.8 us (84%)
  local copies, waits for them, and re-layouts  6.9 us (13%)
  between operations  0.67 us (1%)
    pallas_call x1, Pallas kernels, local(): pl.pallas_call(kernel, out_shape=(jax.ShapeDtypeStruct((NE, 2, 8, NO), BF...  44.8 us
    unnamed x18, local copies, waits for them, and re-layouts  6.9 us

profile of v1, /device:TPU:6, one launch (start us, length us, event | category | flops | bytes accessed | tf_op | source)
XLA Modules:
  0.0 52.4 jit_solution(6789985306694642762)
XLA Ops:
  0.6 0.0 copy-start.6
  0.6 0.0 copy-start.4
  0.7 0.0 copy-start.5
  0.7 0.6 %copy-done.6 = s32[64]{0:T(128)S(1)} copy-done((s32[64]{0:T(128)S(1)}, s32[64]{0:T(128)}, u32[]{:S(2)}) %copy-start.6) | copy-done | bytes 280
  1.3 0.0 copy-done.4
  1.3 0.0 copy-done.5
  1.3 0.0 copy-start
  1.3 0.9 %copy-done = bf16[1,8,128,128]{3,2,1,0:T(8,128)(2,1)S(1)} copy-done((bf16[1,8,128,128]{3,2,1,0:T(8,128)(2,1)S(1)}, bf16[1,8,128,128]{3,2,1,0:T(8,128)(2,1)}, u32[]{:S(2)}) %copy-start) | copy-done | bytes 262168
  2.3 0.0 copy-start.1
  2.3 0.9 %copy-done.1 = bf16[1,8,128,128]{3,2,1,0:T(8,128)(2,1)S(1)} copy-done((bf16[1,8,128,128]{3,2,1,0:T(8,128)(2,1)S(1)}, bf16[1,8,128,128]{3,2,1,0:T(8,128)(2,1)}, u32[]{:S(2)}) %copy-start.1) | copy-done | bytes 262168
  3.2 0.0 copy-start.2
  3.2 0.9 %copy-done.2 = bf16[1,8,128,128]{3,2,1,0:T(8,128)(2,1)S(1)} copy-done((bf16[1,8,128,128]{3,2,1,0:T(8,128)(2,1)S(1)}, bf16[1,8,128,128]{3,2,1,0:T(8,128)(2,1)}, u32[]{:S(2)}) %copy-start.2) | copy-done | bytes 262168
  4.2 0.0 copy-start.3
  4.2 0.9 %copy-done.3 = bf16[8,128,128]{2,1,0:T(8,128)(2,1)S(1)} copy-done((bf16[8,128,128]{2,1,0:T(8,128)(2,1)S(1)}, bf16[8,128,128]{2,1,0:T(8,128)(2,1)}, u32[]{:S(2)}) %copy-start.3) | copy-done | bytes 262168
  5.1 44.8 %born_step.1 = (bf16[64,2,8,128]{3,2,1,0:T(8,128)(2,1)S(1)}, bf16[64,2,8,128]{3,2,1,0:T(8,128)(2,1)S(1)}, f32[1,8]{1,0:T(1,128)S(1)}, f32[1,8]{1,0:T(1,128)S(1)}) custom-call(bf16[8,128,128]{2,1,0:T(8,128)(2,1)S(1)} %bitcast.7, bf16[8,128,128]{2,1,0:T(8,128)(2,1)S(1)} %bitcast.8, bf16[8,128,128]{2,1,0:T(8,128)(2,1)S(1)} %bitcast.9, ...), custom_call_target="tpu_custom_call" | custom-call | tf_op jit(solution)/shard_map/born_step/pallas_call | solution.py:269
  50.0 0.7 %copy.15 = bf16[64,8,2,128]{3,2,1,0:T(2,128)(2,1)} copy(bf16[64,8,2,128]{3,2,1,0:T(2,128)(2,1)S(1)} %bitcast.6) | data formatting | bytes 524288
  50.7 0.7 %copy.16 = bf16[64,8,2,128]{3,2,1,0:T(2,128)(2,1)} copy(bf16[64,8,2,128]{3,2,1,0:T(2,128)(2,1)S(1)} %bitcast.5) | data formatting | bytes 524288
  51.4 0.5 copy.17
  51.9 0.5 copy.18
Async XLA Ops:
  0.6 0.7 %copy-start.6 = (s32[64]{0:T(128)S(1)}, s32[64]{0:T(128)}, u32[]{:S(2)}) copy-start(s32[64]{0:T(128)} %active_ref.1) | copy-start | bytes 772
  0.6 0.7 %copy-start.4 = (f32[2,128]{1,0:T(2,128)S(1)}, f32[2,128]{1,0:T(2,128)}, u32[]{:S(2)}) copy-start(f32[2,128]{1,0:T(2,128)} %pc_ref.1) | copy-start | bytes 3076
  0.7 0.7 %copy-start.5 = (s32[2]{0:T(128)S(1)}, s32[2]{0:T(128)}, u32[]{:S(2)}) copy-start(s32[2]{0:T(128)} %shift_ref.1) | copy-start | bytes 28
  1.3 1.0 %copy-start = (bf16[1,8,128,128]{3,2,1,0:T(8,128)(2,1)S(1)}, bf16[1,8,128,128]{3,2,1,0:T(8,128)(2,1)}, u32[]{:S(2)}) copy-start(bf16[1,8,128,128]{3,2,1,0:T(8,128)(2,1)} %param.7) | copy-start | bytes 786436
  2.3 0.9 %copy-start.1 = (bf16[1,8,128,128]{3,2,1,0:T(8,128)(2,1)S(1)}, bf16[1,8,128,128]{3,2,1,0:T(8,128)(2,1)}, u32[]{:S(2)}) copy-start(bf16[1,8,128,128]{3,2,1,0:T(8,128)(2,1)} %param.8) | copy-start | bytes 786436
  3.2 0.9 %copy-start.2 = (bf16[1,8,128,128]{3,2,1,0:T(8,128)(2,1)S(1)}, bf16[1,8,128,128]{3,2,1,0:T(8,128)(2,1)}, u32[]{:S(2)}) copy-start(bf16[1,8,128,128]{3,2,1,0:T(8,128)(2,1)} %param.9) | copy-start | bytes 786436
  4.2 0.9 %copy-start.3 = (bf16[8,128,128]{2,1,0:T(8,128)(2,1)S(1)}, bf16[8,128,128]{2,1,0:T(8,128)(2,1)}, u32[]{:S(2)}) copy-start(bf16[8,128,128]{2,1,0:T(8,128)(2,1)} %c_ref.1) | copy-start | bytes 786436

commit v2 on v1

--- a/solution.py
+++ b/solution.py
@@ -37,8 +37,9 @@
 
 
 def kernel(
-    g_ref, pl_ref, pg_ref, c_ref, pc_ref, shift_ref, active_ref,
+    g_hbm, pl_hbm, pg_hbm, c_hbm, pc_hbm, shift_hbm, active_hbm,
     sl_ref, sg_ref, cur_ref, ldos_ref,
+    g_ref, pl_ref, pg_ref, c_ref, pc_ref, shift_ref, active_ref, in_sem,
     bare, ct, up_out, up_in, rows, send, recv_low, recv_high, part, total,
     halo_send, halo_recv, x_send, x_recv, t_send, t_recv,
 ):
@@ -47,11 +48,26 @@
     spaces = lax.axis_size("space")
     recvs = (recv_low, recv_high)
 
+    fetches = [
+        pltpu.make_async_copy(source, target, in_sem.at[i])
+        for i, (source, target) in enumerate((
+            (g_hbm, g_ref), (pl_hbm, pl_ref), (pg_hbm, pg_ref), (c_hbm, c_ref),
+            (pc_hbm, pc_ref), (shift_hbm, shift_ref), (active_hbm, active_ref),
+        ))
+    ]
+    for fetch in fetches:
+        fetch.start()
+
+    z, y = me // SIDE, me % SIDE
+    in_y = [lax.rem(y + k, SIDE) for k in range(SIDE)]
+    in_z = [lax.rem(z + k, SIDE) * SIDE for k in range(SIDE)]
+    steps = (1, 7, 2, 6, 3, 5, 4, 0)
+    peers = [in_z[(dy + j) % SIDE] + in_y[dy] for j in (4, 0, 2, 6, 1, 5, 3, 7) for dy in steps if j or dy]
+
     barrier = pltpu.get_barrier_semaphore()
 
-    @pl.loop(1, NE)
-    def _(k):
-        pl.semaphore_signal(barrier, inc=1, device_id={"energy": (me + k) % NE}, device_id_type=MESH)
+    for p in peers:
+        pl.semaphore_signal(barrier, inc=1, device_id={"energy": p}, device_id_type=MESH)
 
     @pl.when(space > 0)
     def _():
@@ -82,6 +98,8 @@
     for g in range(2):
         recvs[g][0:PAD] = jnp.zeros((PAD, 16, NO), BF16)
         recvs[g][PAD + NE :] = jnp.zeros((PAD, 16, NO), BF16)
+    for fetch in fetches:
+        fetch.wait()
     for b in range(NB):
         ct[b] = c_ref[b].T
 
@@ -146,8 +164,7 @@
                 rows[g, pl.ds(start, NE, stride=16), :] = result[at : at + NE]
         return jnp.where(sub8 == b, jnp.broadcast_to(trace, (8, NO)), ldos)
 
-    def exchange(g, k):
-        p = (me + k) % NE
+    def exchange(g, p):
         return pltpu.make_async_remote_copy(
             src_ref=send.at[g, p], dst_ref=recvs[g].at[PAD + me], send_sem=x_send.at[g], recv_sem=x_recv.at[g],
             device_id={"energy": p}, device_id_type=MESH,
@@ -155,11 +172,8 @@
 
     def send_half(g):
         send[g] = rows[g].reshape(NE, 16, NO).astype(BF16)
-
-        @pl.loop(1, NE)
-        def _(k):
-            exchange(g, k).start()
-
+        for p in peers:
+            exchange(g, p).start()
         recvs[g][PAD + me] = send[g, me]
 
     def whole(g):
@@ -220,7 +234,6 @@
     sigma(1)
     sigma(0)
 
-    z, y = me // SIDE, me % SIDE
     value = part[pl.ds(0, 8, stride=2), :] + part[pl.ds(1, 8, stride=2), :]
     for phase in range(2):
         mine = y if phase == 0 else z
@@ -260,11 +273,19 @@
     whole(0).wait_send()
 
 
+def keep(*refs):
+    copies = [pltpu.make_async_copy(refs[i], refs[4 + i], refs[8].at[i]) for i in range(4)]
+    for copy in copies:
+        copy.start()
+    for copy in copies:
+        copy.wait()
+
+
 def local(
     green_ret, prior_less, prior_great, coupling, phonon_coupling, phonon_shift, active_blocks
 ):
     vmem = pl.BlockSpec(memory_space=pltpu.VMEM)
-    smem = pl.BlockSpec(memory_space=pltpu.SMEM)
+    hbm = pl.BlockSpec(memory_space=pltpu.HBM)
     dma = pltpu.SemaphoreType.DMA
     sigma_l, sigma_g, current, ldos = pl.pallas_call(
         kernel,
@@ -274,9 +295,17 @@
             jax.ShapeDtypeStruct((1, NB), F32),
             jax.ShapeDtypeStruct((1, NB), F32),
         ),
-        in_specs=[vmem] * 5 + [smem] * 2,
+        in_specs=[hbm] * 7,
         out_specs=[vmem] * 4,
         scratch_shapes=[
+            pltpu.VMEM((NB, NO, NO), BF16),
+            pltpu.VMEM((NB, NO, NO), BF16),
+            pltpu.VMEM((NB, NO, NO), BF16),
+            pltpu.VMEM((NB, NO, NO), BF16),
+            pltpu.VMEM((2, NO), F32),
+            pltpu.SMEM((2,), jnp.int32),
+            pltpu.SMEM((NE,), jnp.int32),
+            dma((7,)),
             pltpu.VMEM((NB + 1, 2 * NO, NO), BF16),
             pltpu.VMEM((NB, NO, NO), BF16),
             pltpu.VMEM((2 * NO, NO), BF16),
@@ -290,7 +319,7 @@
             dma((2,)), dma((2,)), dma((2,)), dma((2,)), dma((2,)), dma((2,)),
         ],
         compiler_params=pltpu.CompilerParams(
-            collective_id=0, has_side_effects=True, vmem_limit_bytes=32 << 20
+            collective_id=0, has_side_effects=True, vmem_limit_bytes=60 << 20
         ),
         name="born_step",
     )(
@@ -302,6 +331,15 @@
         phonon_shift,
         active_blocks,
     )
+    results = (sigma_l, sigma_g, current, ldos)
+    sigma_l, sigma_g, current, ldos = pl.pallas_call(
+        keep,
+        out_shape=tuple(jax.ShapeDtypeStruct(r.shape, r.dtype) for r in results),
+        in_specs=[vmem] * 4,
+        out_specs=[hbm] * 4,
+        scratch_shapes=[dma((4,))],
+        name="keep",
+    )(*results)
     shape = (NE, NB, 2, NO)
     return sigma_l.reshape(shape), sigma_g.reshape(shape), current, ldos
 

time: 53.1 us -> 49.4 us (0.930)
  local copies, waits for them, and re-layouts: 6.9 us -> 0 us
  Pallas kernels: 44.8 us -> 48.4 us
    unnamed x18 -> x0, local copies, waits for them, and re-layouts: 6.9 us -> none
    pallas_call x0 -> x1, Pallas kernels: none -> 1.86 us  [local(): pl.pallas_call(keep, out_shape=tuple((jax.ShapeDtypeStruct(r.shape, r.dty...]
    pallas_call x1, Pallas kernels: 44.8 us -> 46.6 us  [local(): pl.pallas_call(kernel, out_shape=(jax.ShapeDtypeStruct((NE, 2, 8, NO), BF...]
where the time goes in v2:
time: 49.4 us; the launch traced here: 49.1 us
  Pallas kernels  48.4 us (98%)
  between operations  0.64 us (1%)
    pallas_call x1, Pallas kernels, local(): pl.pallas_call(kernel, out_shape=(jax.ShapeDtypeStruct((NE, 2, 8, NO), BF...  46.6 us
    pallas_call x1, Pallas kernels, local(): pl.pallas_call(keep, out_shape=tuple((jax.ShapeDtypeStruct(r.shape, r.dty...  1.86 us

profile of v2, /device:TPU:6, one launch (start us, length us, event | category | flops | bytes accessed | tf_op | source)
XLA Modules:
  0.0 49.1 jit_solution(7092248365112184035)
XLA Ops:
  0.6 46.6 %born_step.1 = (bf16[64,2,8,128]{3,2,1,0:T(8,128)(2,1)}, bf16[64,2,8,128]{3,2,1,0:T(8,128)(2,1)}, f32[1,8]{1,0:T(1,128)}, f32[1,8]{1,0:T(1,128)}) custom-call(bf16[8,128,128]{2,1,0:T(8,128)(2,1)} %bitcast.5, bf16[8,128,128]{2,1,0:T(8,128)(2,1)} %bitcast.6, bf16[8,128,128]{2,1,0:T(8,128)(2,1)} %bitcast.7, bf16[8,128,128]{2,1,0:T(8,128)(2,1)} %c_hbm.1, ...), custom_call_target="tpu_custom_call" | custom-call | tf_op jit(solution)/shard_map/born_step/pallas_call | solution.py:290
  47.2 1.9 %keep.1 = (bf16[64,2,8,128]{3,2,1,0:T(8,128)(2,1)}, bf16[64,2,8,128]{3,2,1,0:T(8,128)(2,1)}, f32[1,8]{1,0:T(1,128)}, f32[1,8]{1,0:T(1,128)}) custom-call(bf16[64,2,8,128]{3,2,1,0:T(8,128)(2,1)} %get-tuple-element.12.refs_0_, bf16[64,2,8,128]{3,2,1,0:T(8,128)(2,1)} %get-tuple-element.13.refs_1_, f32[1,8]{1,0:T(1,128)} %get-tuple-element.14.refs_2_, ...), custom_call_target="tpu_custom_call" | custom-call | tf_op jit(solution)/shard_map/keep/pallas_call | solution.py:335

commit v3 on v2

--- a/solution.py
+++ b/solution.py
@@ -40,7 +40,7 @@
     g_hbm, pl_hbm, pg_hbm, c_hbm, pc_hbm, shift_hbm, active_hbm,
     sl_ref, sg_ref, cur_ref, ldos_ref,
     g_ref, pl_ref, pg_ref, c_ref, pc_ref, shift_ref, active_ref, in_sem,
-    bare, ct, up_out, up_in, rows, send, recv_low, recv_high, part, total,
+    bare, ct, up_out, up_in, rows, send, recv_low, recv_high, early, part, flows, total,
     halo_send, halo_recv, x_send, x_recv, t_send, t_recv,
 ):
     me = lax.axis_index("energy")
@@ -62,7 +62,9 @@
     in_y = [lax.rem(y + k, SIDE) for k in range(SIDE)]
     in_z = [lax.rem(z + k, SIDE) * SIDE for k in range(SIDE)]
     steps = (1, 7, 2, 6, 3, 5, 4, 0)
-    peers = [in_z[(dy + j) % SIDE] + in_y[dy] for j in (4, 0, 2, 6, 1, 5, 3, 7) for dy in steps if j or dy]
+    offsets = [(dy, (dy + j) % SIDE) for j in (4, 0, 2, 6, 1, 5, 3, 7) for dy in steps if j or dy]
+    offsets.sort(key=lambda at: -sum(min(d, SIDE - d) for d in at))
+    peers = [in_z[dz] + in_y[dy] for dy, dz in offsets]
 
     barrier = pltpu.get_barrier_semaphore()
 
@@ -106,37 +108,6 @@
     make_bare(0)
     make_bare(NB - 1)
     up_out[...] = dot(rise(NB - 1), c_ref[NB - 1]).astype(BF16)
-
-    neighbours = (space > 0).astype(jnp.int32) + (space < spaces - 1).astype(jnp.int32)
-    pl.semaphore_wait(barrier, NE - 1 + neighbours)
-
-    down_copy = pltpu.make_async_remote_copy(
-        src_ref=bare.at[0], dst_ref=bare.at[NB], send_sem=halo_send.at[0], recv_sem=halo_recv.at[0],
-        device_id={"space": lax.rem(space + spaces - 1, spaces)}, device_id_type=MESH,
-    )
-    up_copy = pltpu.make_async_remote_copy(
-        src_ref=up_out, dst_ref=up_in, send_sem=halo_send.at[1], recv_sem=halo_recv.at[1],
-        device_id={"space": lax.rem(space + 1, spaces)}, device_id_type=MESH,
-    )
-
-    @pl.when(space > 0)
-    def _():
-        down_copy.start()
-
-    @pl.when(space < spaces - 1)
-    def _():
-        up_copy.start()
-
-    for b in range(1, NB - 1):
-        make_bare(b)
-
-    @pl.when(space == 0)
-    def _():
-        up_in[...] = jnp.zeros_like(up_in)
-
-    @pl.when(space == spaces - 1)
-    def _():
-        bare[NB] = jnp.zeros((2 * NO, NO), BF16)
 
     open_count = active_ref[me]
     lane8 = lax.broadcasted_iota(jnp.int32, (8, NO), 1)
@@ -156,7 +127,7 @@
         result = dot_t(stacked(half), g_ref[b])
         result = result * jnp.where(space * NB + b < open_count, F32(1), F32(0))
         trace = jnp.sum((result[:NO] + result[NO:]) * diagonal, axis=0, keepdims=True)
-        g, inside = b // HALF, b % HALF
+        g, inside = int(b in (1, 2, 3, 4)), b % HALF
         for kind in range(2):
             for r in range(2):
                 start = kind * 8 + inside * 2 + r
@@ -170,11 +141,12 @@
             device_id={"energy": p}, device_id_type=MESH,
         )
 
-    def send_half(g):
+    def pack(g):
         send[g] = rows[g].reshape(NE, 16, NO).astype(BF16)
-        for p in peers:
+
+    def start(g, targets):
+        for p in targets:
             exchange(g, p).start()
-        recvs[g][PAD + me] = send[g, me]
 
     def whole(g):
         return pltpu.make_async_remote_copy(
@@ -184,22 +156,61 @@
         )
 
     ldos = jnp.zeros((8, NO), F32)
+    for b in range(1, NB - 1):
+        make_bare(b)
+    @pl.when(space == 0)
+    def _():
+        up_in[...] = jnp.zeros_like(up_in)
+
+    @pl.when(space == spaces - 1)
+    def _():
+        bare[NB] = jnp.zeros((2 * NO, NO), BF16)
+
+    for b in (1, 2, 3, 4):
+        ldos = finish(b, ldos)
+    pack(1)
+
+    neighbours = (space > 0).astype(jnp.int32) + (space < spaces - 1).astype(jnp.int32)
+    pl.semaphore_wait(barrier, NE - 1 + neighbours)
+
+    down_copy = pltpu.make_async_remote_copy(
+        src_ref=bare.at[0], dst_ref=bare.at[NB], send_sem=halo_send.at[0], recv_sem=halo_recv.at[0],
+        device_id={"space": lax.rem(space + spaces - 1, spaces)}, device_id_type=MESH,
+    )
+    up_copy = pltpu.make_async_remote_copy(
+        src_ref=up_out, dst_ref=up_in, send_sem=halo_send.at[1], recv_sem=halo_recv.at[1],
+        device_id={"space": lax.rem(space + 1, spaces)}, device_id_type=MESH,
+    )
+
+    @pl.when(space > 0)
+    def _():
+        down_copy.start()
 
     @pl.when(space < spaces - 1)
     def _():
+        up_copy.start()
+
+    start(1, peers[:24])
+    ldos = finish(5, ldos)
+    start(1, peers[24:48])
+    ldos = finish(6, ldos)
+    start(1, peers[48:])
+
+    @pl.when(space < spaces - 1)
+    def _():
         down_copy.wait_recv()
 
-    for b in range(HALF, NB):
-        ldos = finish(b, ldos)
-    send_half(1)
+    ldos = finish(7, ldos)
 
     @pl.when(space > 0)
     def _():
         up_copy.wait_recv()
 
-    for b in range(HALF):
-        ldos = finish(b, ldos)
-    send_half(0)
+    ldos = finish(0, ldos)
+    pack(0)
+    start(0, peers)
+    for g in range(2):
+        recvs[g][PAD + me] = send[g, me]
 
     def as_row(columns):
         sums = jnp.sum(columns, axis=1, keepdims=True)
@@ -212,54 +223,61 @@
     strong, weak = coupling8 * (1 + occupied), coupling8 * occupied
     s0, s1 = shift_ref[0], shift_ref[1]
 
+    first = sub8 < 2
+    place1 = jnp.where(first, sub8 + 8, sub8)
+    place0 = jnp.where(first, sub8, sub8 + 8)
+
     def sigma(g):
         whole(g).wait_recv()
         recv = recvs[g]
 
-        def step(e, acc):
+        def step(e, carry):
             at = PAD + e
             here = recv[at].astype(F32)
             up = recv[at + s0].astype(F32) + recv[at + s1].astype(F32)
             down = recv[at - s0].astype(F32) + recv[at - s1].astype(F32)
-            less = (strong * up[:8] + weak * down[:8]).astype(BF16)
-            great = (strong * down[8:] + weak * up[8:]).astype(BF16)
-            sl_ref[e, g] = less
-            sg_ref[e, g] = great
-            flow = less.astype(F32) * here[8:] - great.astype(F32) * here[:8]
-            sums = jnp.sum(flow, axis=1, keepdims=True)
-            return jnp.where(lane8 == e, sums, acc)
-
-        part[pl.ds(8 * g, 8), :] = lax.fori_loop(0, NE, step, jnp.zeros((8, NO), F32), unroll=8)
+            less = (strong * up[:8] + weak * down[:8]).astype(BF16).astype(F32)
+            great = (strong * down[8:] + weak * up[8:]).astype(BF16).astype(F32)
+            if g == 1:
+                early[0, e] = less
+                early[1, e] = great
+            else:
+                for out, before, now in ((sl_ref, early[0, e], less), (sg_ref, early[1, e], great)):
+                    low = jnp.where(first, now, before)
+                    high = jnp.where(first, before, now)
+                    out[e] = jnp.concatenate([low, high], axis=0).astype(BF16)
+            flow = less * here[8:] - great * here[:8]
+            sums = jnp.where(lane8 == (place1 if g == 1 else place0), jnp.sum(flow, axis=1, keepdims=True), F32(0))
+            if g == 1:
+                part[e] = sums
+            else:
+                flows[e] = jnp.sum(part[e] + sums, axis=0, keepdims=True)
+            return carry
+
+        lax.fori_loop(0, NE, step, 0, unroll=8)
 
     sigma(1)
     sigma(0)
 
-    value = part[pl.ds(0, 8, stride=2), :] + part[pl.ds(1, 8, stride=2), :]
-    for phase in range(2):
-        mine = y if phase == 0 else z
-        total[phase, mine] = value
-
-        def hop(k, phase=phase, mine=mine):
-            there = (mine + k) % SIDE
-            peer = z * SIDE + there if phase == 0 else there * SIDE + y
-            return pltpu.make_async_remote_copy(
-                src_ref=total.at[phase, mine], dst_ref=total.at[phase, mine],
-                send_sem=t_send.at[phase], recv_sem=t_recv.at[phase],
-                device_id={"energy": peer}, device_id_type=MESH,
-            )
-
-        for k in range(1, SIDE):
-            hop(k).start()
-        everything = pltpu.make_async_remote_copy(
-            src_ref=total.at[phase, pl.ds(0, SIDE - 1)], dst_ref=total.at[phase, pl.ds(0, SIDE - 1)],
-            send_sem=t_send.at[phase], recv_sem=t_recv.at[phase],
-            device_id={"energy": (me + 1) % NE}, device_id_type=MESH,
+    def share(p):
+        return pltpu.make_async_remote_copy(
+            src_ref=flows.at[p], dst_ref=total.at[me], send_sem=t_send, recv_sem=t_recv,
+            device_id={"energy": p}, device_id_type=MESH,
         )
-        everything.wait_recv()
-        value = jnp.sum(total[phase], axis=0)
-        everything.wait_send()
-
-    cur_ref[...] = as_row(jnp.where(lane8 == me, value, F32(0))) / NO
+
+    for p in peers:
+        share(p).start()
+    total[me] = flows[me]
+    shares = pltpu.make_async_remote_copy(
+        src_ref=flows.at[pl.ds(0, NE - 1)], dst_ref=total.at[pl.ds(0, NE - 1)], send_sem=t_send, recv_sem=t_recv,
+        device_id={"energy": peers[0]}, device_id_type=MESH,
+    )
+    shares.wait_recv()
+    lanes = [total[e] for e in range(NE)]
+    while len(lanes) > 1:
+        lanes = [one + other for one, other in zip(lanes[::2], lanes[1::2])]
+    cur_ref[...] = as_row(jnp.where(lane8 // 2 == sub8, jnp.broadcast_to(lanes[0], (8, NO)), F32(0))) / NO
+    shares.wait_send()
 
     @pl.when(space > 0)
     def _():
@@ -290,8 +308,8 @@
     sigma_l, sigma_g, current, ldos = pl.pallas_call(
         kernel,
         out_shape=(
-            jax.ShapeDtypeStruct((NE, 2, 8, NO), BF16),
-            jax.ShapeDtypeStruct((NE, 2, 8, NO), BF16),
+            jax.ShapeDtypeStruct((NE, 2 * NB, NO), BF16),
+            jax.ShapeDtypeStruct((NE, 2 * NB, NO), BF16),
             jax.ShapeDtypeStruct((1, NB), F32),
             jax.ShapeDtypeStruct((1, NB), F32),
         ),
@@ -314,9 +332,11 @@
             pltpu.VMEM((2, NE, 16, NO), BF16),
             pltpu.VMEM((NE + 2 * PAD, 16, NO), BF16),
             pltpu.VMEM((NE + 2 * PAD, 16, NO), BF16),
-            pltpu.VMEM((16, NO), F32),
-            pltpu.VMEM((2, SIDE, 8, NO), F32),
-            dma((2,)), dma((2,)), dma((2,)), dma((2,)), dma((2,)), dma((2,)),
+            pltpu.VMEM((2, NE, 8, NO), F32),
+            pltpu.VMEM((NE, 8, NO), F32),
+            pltpu.VMEM((NE, 1, NO), F32),
+            pltpu.VMEM((NE, 1, NO), F32),
+            dma((2,)), dma((2,)), dma((2,)), dma((2,)), dma, dma,
         ],
         compiler_params=pltpu.CompilerParams(
             collective_id=0, has_side_effects=True, vmem_limit_bytes=60 << 20

time: 49.4 us -> 42.2 us (0.85)
  Pallas kernels: 48.4 us -> 41.4 us
    pallas_call x1, Pallas kernels: 46.6 us -> 39.5 us  [local(): pl.pallas_call(kernel, out_shape=(jax.ShapeDtypeStruct((NE, 2 * NB, NO),...]
where the time goes in v3:
time: 42.2 us; the launch traced here: 42 us
  Pallas kernels  41.4 us (98%)
  between operations  0.64 us (2%)
    pallas_call x1, Pallas kernels, local(): pl.pallas_call(kernel, out_shape=(jax.ShapeDtypeStruct((NE, 2 * NB, NO),...  39.5 us
    pallas_call x1, Pallas kernels, local(): pl.pallas_call(keep, out_shape=tuple((jax.ShapeDtypeStruct(r.shape, r.dty...  1.86 us

profile of v3, /device:TPU:6, one launch (start us, length us, event | category | flops | bytes accessed | tf_op | source)
XLA Modules:
  0.0 42.0 jit_solution(7423089529809736939)
XLA Ops:
  0.6 39.5 %born_step.1 = (bf16[64,16,128]{2,1,0:T(8,128)(2,1)}, bf16[64,16,128]{2,1,0:T(8,128)(2,1)}, f32[1,8]{1,0:T(1,128)}, f32[1,8]{1,0:T(1,128)}) custom-call(bf16[8,128,128]{2,1,0:T(8,128)(2,1)} %bitcast.5, bf16[8,128,128]{2,1,0:T(8,128)(2,1)} %bitcast.6, bf16[8,128,128]{2,1,0:T(8,128)(2,1)} %bitcast.7, bf16[8,128,128]{2,1,0:T(8,128)(2,1)} %c_hbm.1, ...), custom_call_target="tpu_custom_call" | custom-call | tf_op jit(solution)/shard_map/born_step/pallas_call | solution.py:308
  40.2 1.9 %keep.1 = (bf16[64,16,128]{2,1,0:T(8,128)(2,1)}, bf16[64,16,128]{2,1,0:T(8,128)(2,1)}, f32[1,8]{1,0:T(1,128)}, f32[1,8]{1,0:T(1,128)}) custom-call(bf16[64,16,128]{2,1,0:T(8,128)(2,1)} %get-tuple-element.12.refs_0_, bf16[64,16,128]{2,1,0:T(8,128)(2,1)} %get-tuple-element.13.refs_1_, f32[1,8]{1,0:T(1,128)} %get-tuple-element.14.refs_2_, ...), custom_call_target="tpu_custom_call" | custom-call | tf_op jit(solution)/shard_map/keep/pallas_call | solution.py:355

commit v4 on v3

--- a/solution.py
+++ b/solution.py
@@ -17,6 +17,7 @@
 NO = 128
 HALF = 4
 PAD = 32
+CUTS = 2
 SIDE = 8
 
 
@@ -40,7 +41,7 @@
     g_hbm, pl_hbm, pg_hbm, c_hbm, pc_hbm, shift_hbm, active_hbm,
     sl_ref, sg_ref, cur_ref, ldos_ref,
     g_ref, pl_ref, pg_ref, c_ref, pc_ref, shift_ref, active_ref, in_sem,
-    bare, ct, up_out, up_in, rows, send, recv_low, recv_high, early, part, flows, total,
+    left, source, half, mixed, bare, ct, up_out, up_in, rows, send, recv_low, recv_high, early, part, flows, total,
     halo_send, halo_recv, x_send, x_recv, t_send, t_recv,
 ):
     me = lax.axis_index("energy")
@@ -55,7 +56,7 @@
             (pc_hbm, pc_ref), (shift_hbm, shift_ref), (active_hbm, active_ref),
         ))
     ]
-    for fetch in fetches:
+    for fetch in fetches[:4]:
         fetch.start()
 
     z, y = me // SIDE, me % SIDE
@@ -79,6 +80,9 @@
     def _():
         pl.semaphore_signal(barrier, inc=1, device_id={"space": space + 1}, device_id_type=MESH)
 
+    for fetch in fetches[4:]:
+        fetch.start()
+
     row_id = lax.broadcasted_iota(jnp.int32, (NO, NO), 0)
     col_id = lax.broadcasted_iota(jnp.int32, (NO, NO), 1)
     original = 2 * (row_id % NE) + row_id // NE
@@ -104,6 +108,7 @@
         fetch.wait()
     for b in range(NB):
         ct[b] = c_ref[b].T
+        mixed[b] = dot(permute, g_ref[b]).astype(BF16)
 
     make_bare(0)
     make_bare(NB - 1)
@@ -113,27 +118,33 @@
     lane8 = lax.broadcasted_iota(jnp.int32, (8, NO), 1)
     sub8 = lax.broadcasted_iota(jnp.int32, (8, NO), 0)
 
-    def finish(b, ldos):
-        fall = stacked(dot(c_ref[b], side_by_side(bare[b + 1])).astype(BF16))
-        if b == 0:
-            hops = dot(fall, ct[0]) + up_in[...].astype(F32)
-        else:
-            left = jnp.concatenate([rise(b - 1), fall], axis=1)
-            right = jnp.concatenate([c_ref[b - 1], ct[b]], axis=0)
-            hops = dot(left, right)
-        source = (prior(b).astype(F32) + hops).astype(BF16)
-        mine = dot(permute, g_ref[b]).astype(BF16)
-        half = dot(mine, side_by_side(source)).astype(BF16)
-        result = dot_t(stacked(half), g_ref[b])
-        result = result * jnp.where(space * NB + b < open_count, F32(1), F32(0))
-        trace = jnp.sum((result[:NO] + result[NO:]) * diagonal, axis=0, keepdims=True)
-        g, inside = int(b in (1, 2, 3, 4)), b % HALF
-        for kind in range(2):
-            for r in range(2):
-                start = kind * 8 + inside * 2 + r
-                at = kind * NO + r * NE
-                rows[g, pl.ds(start, NE, stride=16), :] = result[at : at + NE]
-        return jnp.where(sub8 == b, jnp.broadcast_to(trace, (8, NO)), ldos)
+    def finish(blocks, ldos):
+        for b in blocks:
+            fall = stacked(dot(c_ref[b], side_by_side(bare[b + 1])).astype(BF16))
+            if b == 0:
+                left[0, :, :NO] = fall
+            else:
+                left[b] = jnp.concatenate([rise(b - 1), fall], axis=1)
+        for b in blocks:
+            if b == 0:
+                hops = dot(left[0, :, :NO], ct[0]) + up_in[...].astype(F32)
+            else:
+                hops = dot(left[b], jnp.concatenate([c_ref[b - 1], ct[b]], axis=0))
+            source[b] = side_by_side((prior(b).astype(F32) + hops).astype(BF16))
+        for b in blocks:
+            half[b] = stacked(dot(mixed[b], source[b]).astype(BF16))
+        for b in blocks:
+            result = dot_t(half[b], g_ref[b])
+            result = result * jnp.where(space * NB + b < open_count, F32(1), F32(0))
+            trace = jnp.sum((result[:NO] + result[NO:]) * diagonal, axis=0, keepdims=True)
+            g, inside = int(b in (1, 2, 3, 4)), b % HALF
+            for kind in range(2):
+                for r in range(2):
+                    begin = kind * 8 + inside * 2 + r
+                    at = kind * NO + r * NE
+                    rows[g, pl.ds(begin, NE, stride=16), :] = result[at : at + NE]
+            ldos = jnp.where(sub8 == b, jnp.broadcast_to(trace, (8, NO)), ldos)
+        return ldos
 
     def exchange(g, p):
         return pltpu.make_async_remote_copy(
@@ -166,8 +177,7 @@
     def _():
         bare[NB] = jnp.zeros((2 * NO, NO), BF16)
 
-    for b in (1, 2, 3, 4):
-        ldos = finish(b, ldos)
+    ldos = finish((1, 2, 3, 4), ldos)
     pack(1)
 
     neighbours = (space > 0).astype(jnp.int32) + (space < spaces - 1).astype(jnp.int32)
@@ -190,23 +200,18 @@
     def _():
         up_copy.start()
 
-    start(1, peers[:24])
-    ldos = finish(5, ldos)
-    start(1, peers[24:48])
-    ldos = finish(6, ldos)
-    start(1, peers[48:])
+    start(1, peers)
 
     @pl.when(space < spaces - 1)
     def _():
         down_copy.wait_recv()
 
-    ldos = finish(7, ldos)
 
     @pl.when(space > 0)
     def _():
         up_copy.wait_recv()
 
-    ldos = finish(0, ldos)
+    ldos = finish((5, 6, 7, 0), ldos)
     pack(0)
     start(0, peers)
     for g in range(2):
@@ -238,14 +243,8 @@
             down = recv[at - s0].astype(F32) + recv[at - s1].astype(F32)
             less = (strong * up[:8] + weak * down[:8]).astype(BF16).astype(F32)
             great = (strong * down[8:] + weak * up[8:]).astype(BF16).astype(F32)
-            if g == 1:
-                early[0, e] = less
-                early[1, e] = great
-            else:
-                for out, before, now in ((sl_ref, early[0, e], less), (sg_ref, early[1, e], great)):
-                    low = jnp.where(first, now, before)
-                    high = jnp.where(first, before, now)
-                    out[e] = jnp.concatenate([low, high], axis=0).astype(BF16)
+            early[g, 0, e] = less
+            early[g, 1, e] = great
             flow = less * here[8:] - great * here[:8]
             sums = jnp.where(lane8 == (place1 if g == 1 else place0), jnp.sum(flow, axis=1, keepdims=True), F32(0))
             if g == 1:
@@ -254,7 +253,7 @@
                 flows[e] = jnp.sum(part[e] + sums, axis=0, keepdims=True)
             return carry
 
-        lax.fori_loop(0, NE, step, 0, unroll=8)
+        lax.fori_loop(0, NE, step, 0, unroll=32)
 
     sigma(1)
     sigma(0)
@@ -268,6 +267,15 @@
     for p in peers:
         share(p).start()
     total[me] = flows[me]
+
+    def merge(e, carry):
+        for kind, out in enumerate((sl_ref, sg_ref)):
+            low = jnp.where(first, early[0, kind, e], early[1, kind, e])
+            high = jnp.where(first, early[1, kind, e], early[0, kind, e])
+            out[e] = jnp.concatenate([low, high], axis=0).astype(BF16)
+        return carry
+
+    lax.fori_loop(0, NE, merge, 0, unroll=8)
     shares = pltpu.make_async_remote_copy(
         src_ref=flows.at[pl.ds(0, NE - 1)], dst_ref=total.at[pl.ds(0, NE - 1)], send_sem=t_send, recv_sem=t_recv,
         device_id={"energy": peers[0]}, device_id_type=MESH,
@@ -292,7 +300,12 @@
 
 
 def keep(*refs):
-    copies = [pltpu.make_async_copy(refs[i], refs[4 + i], refs[8].at[i]) for i in range(4)]
+    copies = []
+    for i in range(2):
+        for n in range(CUTS):
+            piece = pl.ds(n * (NE // CUTS), NE // CUTS)
+            copies.append(pltpu.make_async_copy(refs[i].at[piece], refs[4 + i].at[piece], refs[8].at[4 + CUTS * i + n]))
+    copies += [pltpu.make_async_copy(refs[i], refs[4 + i], refs[8].at[i]) for i in (2, 3)]
     for copy in copies:
         copy.start()
     for copy in copies:
@@ -324,6 +337,10 @@
             pltpu.SMEM((2,), jnp.int32),
             pltpu.SMEM((NE,), jnp.int32),
             dma((7,)),
+            pltpu.VMEM((NB, 2 * NO, 2 * NO), BF16),
+            pltpu.VMEM((NB, NO, 2 * NO), BF16),
+            pltpu.VMEM((NB, 2 * NO, NO), BF16),
+            pltpu.VMEM((NB, NO, NO), BF16),
             pltpu.VMEM((NB + 1, 2 * NO, NO), BF16),
             pltpu.VMEM((NB, NO, NO), BF16),
             pltpu.VMEM((2 * NO, NO), BF16),
@@ -332,24 +349,29 @@
             pltpu.VMEM((2, NE, 16, NO), BF16),
             pltpu.VMEM((NE + 2 * PAD, 16, NO), BF16),
             pltpu.VMEM((NE + 2 * PAD, 16, NO), BF16),
-            pltpu.VMEM((2, NE, 8, NO), F32),
+            pltpu.VMEM((2, 2, NE, 8, NO), F32),
             pltpu.VMEM((NE, 8, NO), F32),
             pltpu.VMEM((NE, 1, NO), F32),
             pltpu.VMEM((NE, 1, NO), F32),
             dma((2,)), dma((2,)), dma((2,)), dma((2,)), dma, dma,
         ],
         compiler_params=pltpu.CompilerParams(
-            collective_id=0, has_side_effects=True, vmem_limit_bytes=60 << 20
+            collective_id=0, has_side_effects=True, vmem_limit_bytes=32 << 20
         ),
         name="born_step",
     )(
-        green_ret.reshape(NB, NO, NO),
-        prior_less.reshape(NB, NO, NO),
-        prior_great.reshape(NB, NO, NO),
-        coupling,
-        phonon_coupling,
-        phonon_shift,
-        active_blocks,
+        *(
+            pltpu.with_memory_space_constraint(operand, pltpu.HBM)
+            for operand in (
+                green_ret.reshape(NB, NO, NO),
+                prior_less.reshape(NB, NO, NO),
+                prior_great.reshape(NB, NO, NO),
+                coupling,
+                phonon_coupling,
+                phonon_shift,
+                active_blocks,
+            )
+        )
     )
     results = (sigma_l, sigma_g, current, ldos)
     sigma_l, sigma_g, current, ldos = pl.pallas_call(
@@ -357,9 +379,9 @@
         out_shape=tuple(jax.ShapeDtypeStruct(r.shape, r.dtype) for r in results),
         in_specs=[vmem] * 4,
         out_specs=[hbm] * 4,
-        scratch_shapes=[dma((4,))],
+        scratch_shapes=[dma((4 + 2 * CUTS,))],
         name="keep",
-    )(*results)
+    )(*(pltpu.with_memory_space_constraint(r, pltpu.VMEM) for r in results))
     shape = (NE, NB, 2, NO)
     return sigma_l.reshape(shape), sigma_g.reshape(shape), current, ldos
 

time: 42.2 us -> 39.2 us (0.929)
  Pallas kernels: 41.4 us -> 38.4 us
    pallas_call x1, Pallas kernels: 39.5 us -> 37.5 us  [local(): pl.pallas_call(kernel, out_shape=(jax.ShapeDtypeStruct((NE, 2 * NB, NO),...]
    pallas_call x1, Pallas kernels: 1.86 us -> 0.86 us  [local(): pl.pallas_call(keep, out_shape=tuple((jax.ShapeDtypeStruct(r.shape, r.dty...]
where the time goes in v4:
time: 39.2 us; the launch traced here: 39 us
  Pallas kernels  38.4 us (98%)
  between operations  0.64 us (2%)
    pallas_call x1, Pallas kernels, local(): pl.pallas_call(kernel, out_shape=(jax.ShapeDtypeStruct((NE, 2 * NB, NO),...  37.5 us
    pallas_call x1, Pallas kernels, local(): pl.pallas_call(keep, out_shape=tuple((jax.ShapeDtypeStruct(r.shape, r.dty...  0.86 us

profile of v4, /device:TPU:6, one launch (start us, length us, event | category | flops | bytes accessed | tf_op | source)
XLA Modules:
  0.0 39.0 jit_solution(9639851343226135457)
XLA Ops:
  0.6 37.5 %born_step.1 = (bf16[64,16,128]{2,1,0:T(8,128)(2,1)S(1)}, bf16[64,16,128]{2,1,0:T(8,128)(2,1)S(1)}, f32[1,8]{1,0:T(1,128)S(1)}, f32[1,8]{1,0:T(1,128)S(1)}) custom-call(bf16[8,128,128]{2,1,0:T(8,128)(2,1)} %bitcast.5, bf16[8,128,128]{2,1,0:T(8,128)(2,1)} %bitcast.6, bf16[8,128,128]{2,1,0:T(8,128)(2,1)} %bitcast.7, bf16[8,128,128]{2,1,0:T(8,128)(2,1)} %c_hbm.1, ...), custom_call_target="tpu_custom_call" | custom-call | tf_op jit(solution)/shard_map/born_step/pallas_call | solution.py:321
  38.2 0.9 %keep.1 = (bf16[64,16,128]{2,1,0:T(8,128)(2,1)}, bf16[64,16,128]{2,1,0:T(8,128)(2,1)}, f32[1,8]{1,0:T(1,128)}, f32[1,8]{1,0:T(1,128)}) custom-call(bf16[64,16,128]{2,1,0:T(8,128)(2,1)S(1)} %get-tuple-element.12.refs_0_, bf16[64,16,128]{2,1,0:T(8,128)(2,1)S(1)} %get-tuple-element.13.refs_1_, f32[1,8]{1,0:T(1,128)S(1)} %get-tuple-element.14.refs_2_, ...), custom_call_target="tpu_custom_call" | custom-call | tf_op jit(solution)/shard_map/keep/pallas_call | solution.py:377

commit v5 on v4

--- a/solution.py
+++ b/solution.py
@@ -56,8 +56,6 @@
             (pc_hbm, pc_ref), (shift_hbm, shift_ref), (active_hbm, active_ref),
         ))
     ]
-    for fetch in fetches[:4]:
-        fetch.start()
 
     z, y = me // SIDE, me % SIDE
     in_y = [lax.rem(y + k, SIDE) for k in range(SIDE)]
@@ -70,7 +68,7 @@
     barrier = pltpu.get_barrier_semaphore()
 
     for p in peers:
-        pl.semaphore_signal(barrier, inc=1, device_id={"energy": p}, device_id_type=MESH)
+        pl.semaphore_signal(barrier, inc=1, device_id=(p, space), device_id_type=MESH)
 
     @pl.when(space > 0)
     def _():
@@ -80,7 +78,7 @@
     def _():
         pl.semaphore_signal(barrier, inc=1, device_id={"space": space + 1}, device_id_type=MESH)
 
-    for fetch in fetches[4:]:
+    for fetch in fetches:
         fetch.start()
 
     row_id = lax.broadcasted_iota(jnp.int32, (NO, NO), 0)
@@ -149,7 +147,7 @@
     def exchange(g, p):
         return pltpu.make_async_remote_copy(
             src_ref=send.at[g, p], dst_ref=recvs[g].at[PAD + me], send_sem=x_send.at[g], recv_sem=x_recv.at[g],
-            device_id={"energy": p}, device_id_type=MESH,
+            device_id=(p, space), device_id_type=MESH,
         )
 
     def pack(g):
@@ -261,7 +259,7 @@
     def share(p):
         return pltpu.make_async_remote_copy(
             src_ref=flows.at[p], dst_ref=total.at[me], send_sem=t_send, recv_sem=t_recv,
-            device_id={"energy": p}, device_id_type=MESH,
+            device_id=(p, space), device_id_type=MESH,
         )
 
     for p in peers:
@@ -278,7 +276,7 @@
     lax.fori_loop(0, NE, merge, 0, unroll=8)
     shares = pltpu.make_async_remote_copy(
         src_ref=flows.at[pl.ds(0, NE - 1)], dst_ref=total.at[pl.ds(0, NE - 1)], send_sem=t_send, recv_sem=t_recv,
-        device_id={"energy": peers[0]}, device_id_type=MESH,
+        device_id=(peers[0], space), device_id_type=MESH,
     )
     shares.wait_recv()
     lanes = [total[e] for e in range(NE)]

time: 39.2 us -> 39.2 us (level)
  no operation moved by 1% of the time
where the time goes in v5:
time: 39.2 us; the launch traced here: 39 us
  Pallas kernels  38.4 us (98%)
  between operations  0.64 us (2%)
    pallas_call x1, Pallas kernels, local(): pl.pallas_call(kernel, out_shape=(jax.ShapeDtypeStruct((NE, 2 * NB, NO),...  37.5 us
    pallas_call x1, Pallas kernels, local(): pl.pallas_call(keep, out_shape=tuple((jax.ShapeDtypeStruct(r.shape, r.dty...  0.86 us

profile of v5, /device:TPU:6, one launch (start us, length us, event | category | flops | bytes accessed | tf_op | source)
XLA Modules:
  0.0 39.0 jit_solution(3645229605090253531)
XLA Ops:
  0.6 37.5 %born_step.1 = (bf16[64,16,128]{2,1,0:T(8,128)(2,1)S(1)}, bf16[64,16,128]{2,1,0:T(8,128)(2,1)S(1)}, f32[1,8]{1,0:T(1,128)S(1)}, f32[1,8]{1,0:T(1,128)S(1)}) custom-call(bf16[8,128,128]{2,1,0:T(8,128)(2,1)} %bitcast.5, bf16[8,128,128]{2,1,0:T(8,128)(2,1)} %bitcast.6, bf16[8,128,128]{2,1,0:T(8,128)(2,1)} %bitcast.7, bf16[8,128,128]{2,1,0:T(8,128)(2,1)} %c_hbm.1, ...), custom_call_target="tpu_custom_call" | custom-call | tf_op jit(solution)/shard_map/born_step/pallas_call | solution.py:319
  38.2 0.9 %keep.1 = (bf16[64,16,128]{2,1,0:T(8,128)(2,1)}, bf16[64,16,128]{2,1,0:T(8,128)(2,1)}, f32[1,8]{1,0:T(1,128)}, f32[1,8]{1,0:T(1,128)}) custom-call(bf16[64,16,128]{2,1,0:T(8,128)(2,1)S(1)} %get-tuple-element.12.refs_0_, bf16[64,16,128]{2,1,0:T(8,128)(2,1)S(1)} %get-tuple-element.13.refs_1_, f32[1,8]{1,0:T(1,128)S(1)} %get-tuple-element.14.refs_2_, ...), custom_call_target="tpu_custom_call" | custom-call | tf_op jit(solution)/shard_map/keep/pallas_call | solution.py:375

commit v6 on v5

--- a/solution.py
+++ b/solution.py
@@ -251,7 +251,7 @@
                 flows[e] = jnp.sum(part[e] + sums, axis=0, keepdims=True)
             return carry
 
-        lax.fori_loop(0, NE, step, 0, unroll=32)
+        lax.fori_loop(0, NE, step, 0, unroll=64)
 
     sigma(1)
     sigma(0)

time: 39.2 us -> 39.1 us (level)
  no operation moved by 1% of the time
where the time goes in v6:
time: 39.1 us; the launch traced here: 39 us
  Pallas kernels  38.3 us (98%)
  between operations  0.64 us (2%)
    pallas_call x1, Pallas kernels, local(): pl.pallas_call(kernel, out_shape=(jax.ShapeDtypeStruct((NE, 2 * NB, NO),...  37.5 us
    pallas_call x1, Pallas kernels, local(): pl.pallas_call(keep, out_shape=tuple((jax.ShapeDtypeStruct(r.shape, r.dty...  0.86 us

profile of v6, /device:TPU:6, one launch (start us, length us, event | category | flops | bytes accessed | tf_op | source)
XLA Modules:
  0.0 39.0 jit_solution(3177695552061912625)
XLA Ops:
  0.6 37.5 %born_step.1 = (bf16[64,16,128]{2,1,0:T(8,128)(2,1)S(1)}, bf16[64,16,128]{2,1,0:T(8,128)(2,1)S(1)}, f32[1,8]{1,0:T(1,128)S(1)}, f32[1,8]{1,0:T(1,128)S(1)}) custom-call(bf16[8,128,128]{2,1,0:T(8,128)(2,1)} %bitcast.5, bf16[8,128,128]{2,1,0:T(8,128)(2,1)} %bitcast.6, bf16[8,128,128]{2,1,0:T(8,128)(2,1)} %bitcast.7, bf16[8,128,128]{2,1,0:T(8,128)(2,1)} %c_hbm.1, ...), custom_call_target="tpu_custom_call" | custom-call | tf_op jit(solution)/shard_map/born_step/pallas_call | solution.py:319
  38.1 0.9 %keep.1 = (bf16[64,16,128]{2,1,0:T(8,128)(2,1)}, bf16[64,16,128]{2,1,0:T(8,128)(2,1)}, f32[1,8]{1,0:T(1,128)}, f32[1,8]{1,0:T(1,128)}) custom-call(bf16[64,16,128]{2,1,0:T(8,128)(2,1)S(1)} %get-tuple-element.12.refs_0_, bf16[64,16,128]{2,1,0:T(8,128)(2,1)S(1)} %get-tuple-element.13.refs_1_, f32[1,8]{1,0:T(1,128)S(1)} %get-tuple-element.14.refs_2_, ...), custom_call_target="tpu_custom_call" | custom-call | tf_op jit(solution)/shard_map/keep/pallas_call | solution.py:375
